TPU v7x, 128 devices: a whole 4x4x4 slice. The times are simulated.
128 devices in a mesh: row: 16 (over x, y), col: 4 (over z), layer: 2 (over core).
Axes of the slice: x: 4, y: 4, z: 4, core: 2. Of those that a mesh axis runs over, the one named last changes fastest.
Arguments:
- density: float32 [4096, 4096], P('row', ('col', 'layer')), may hold values from -2 to 2
- masks: int32 [6, 64, 64], replicated, may hold values from 0 to 1, as said below
- branch: int32 [5], replicated, may hold values from 0 to 1, as said below
- perm: int32 [64], replicated, may hold values from 0 to 63, each once
Outputs:
- purified: float32 [4096, 4096], P('row', ('col', 'layer'))
Inputs may be any that keep to these rules, and one draw needn't show every extreme that they name: masks are symmetric in their last two dimensions, every diagonal block is occupied, and block (i, j) of masks[s] is occupied only where the cyclic distance between i and j is at most 6 + s. `branch`: both values occur among the steps. `perm`: a permutation of 0..63.
All inputs are finite; a program needn't handle non-finite values.
Results may differ from a plain program's by a relative error of at most 0.0003.
Values sent between devices are 32-bit elements; how exact they have to be, the bound alone decides.
No kernel may reach another device: no remote copies, remote signals or barrier semaphores. Data moves between devices by JAX's collectives and lax.ppermute only.
A program may use at most 64 MiB of HBM per device.

v0:
```python
import jax
import jax.numpy as jnp
from jax import lax
from jax.sharding import PartitionSpec as P

BS = 64
STEPS = 5


def expand(block_mask):
    grown = jnp.repeat(block_mask, BS, axis=0)
    return jnp.repeat(grown, BS, axis=1).astype(jnp.float32)


def shards(density, masks, branch, perm):
    rows_here = density.shape[0]
    cols_here = density.shape[1]
    row_blocks = rows_here // BS
    col_blocks = cols_here // BS
    row_start = lax.axis_index("row") * row_blocks
    col_start = lax.axis_index(("col", "layer")) * col_blocks
    row_ids = lax.dynamic_slice_in_dim(perm, row_start, row_blocks)
    col_ids = lax.dynamic_slice_in_dim(perm, col_start, col_blocks)
    local_masks = jnp.take(jnp.take(masks, row_ids, axis=1), col_ids, axis=2)
    current = density * expand(local_masks[0])
    for step in range(STEPS):
        panel = lax.all_gather(current, ("col", "layer"), axis=1, tiled=True)
        square = jnp.dot(
            panel,
            lax.all_gather(current, "row", axis=0, tiled=True),
            preferred_element_type=jnp.float32,
            precision=lax.Precision.HIGHEST,
        )
        picked = jnp.where(branch[step] == 1, 2.0 * current - square, square)
        current = picked * expand(local_masks[step + 1])
    return current


def solution(mesh):
    return jax.shard_map(
        shards,
        mesh=mesh,
        in_specs=(P("row", ("col", "layer")), P(), P(), P()),
        out_specs=P("row", ("col", "layer")),
        check_vma=False,
    )
```

profile of v0, /device:TPU:1, one launch (start us, length us, event | category | flops | bytes accessed | tf_op | source)
XLA Modules:
  0.0 603.6 jit_solution(2125554987655784131)
XLA Ops:
  6.5 0.8 compare_and_fusion
  7.5 0.6 gather_fusion
  8.3 0.7 compare_and_fusion.1
  9.0 0.6 gather_fusion.1
  10.2 1.9 mul.45
  12.2 0.7 all-gather.13.cloned.1.call-update
  13.5 1.5 fusion.11
  15.5 32.8 %all-gather.11.cloned.1.call-done = f32[256,4096]{1,0:T(8,128)} async-done(((f32[256,512]{1,0:T(8,128)}), f32[256,4096]{1,0:T(8,128)}) %all-gather.11.cloned.1.call-update) | async-done | bytes 4194320 | tf_op jit(solution)/shard_map/all_gather | solution.py:27
  48.3 72.2 %all-gather.13.cloned.1.call-done = f32[4096,512]{1,0:T(8,128)} async-done(((f32[256,512]{1,0:T(8,128)}), f32[4096,512]{1,0:T(8,128)}) %all-gather.13.cloned.1.call-update) | async-done | bytes 8388624 | tf_op jit(solution)/shard_map/all_gather | solution.py:30
  120.5 11.5 %fusion = f32[256,512]{1,0:T(8,128)} fusion(f32[256,512]{1,0:T(8,128)S(1)} %copy.29, f32[256,512]{1,0:T(8,128)} %mul.45, pred[]{:T(512)} %bitcast.4, f32[256,4096]{1,0:T(8,128)} %all-gather.11.cloned.1.call-done, f32[4096,512]{1,0:T(8,128)} %all-gather.13.cloned.1.call-done), kind=kOutput, calls=%fused_computation.7 | convolution fusion | flops 6442975232 | bytes 14155777 | tf_op jit(solution)/shard_map/dot_general | solution.py:28
  132.0 0.5 all-gather.17.cloned.1.call-update
  133.8 30.8 %all-gather.15.cloned.1.call-done = f32[256,4096]{1,0:T(8,128)} async-done(((f32[256,512]{1,0:T(8,128)}), f32[256,4096]{1,0:T(8,128)}) %all-gather.15.cloned.1.call-update) | async-done | bytes 4194320 | tf_op jit(solution)/shard_map/all_gather | solution.py:27
  164.6 72.0 %all-gather.17.cloned.1.call-done = f32[4096,512]{1,0:T(8,128)} async-done(((f32[256,512]{1,0:T(8,128)}), f32[4096,512]{1,0:T(8,128)}) %all-gather.17.cloned.1.call-update) | async-done | bytes 8388624 | tf_op jit(solution)/shard_map/all_gather | solution.py:30
  236.6 11.5 %fusion.1 = f32[256,512]{1,0:T(8,128)} fusion(f32[256,512]{1,0:T(8,128)S(1)} %copy.31, f32[256,512]{1,0:T(8,128)} %fusion, pred[]{:T(512)} %bitcast.3, f32[256,4096]{1,0:T(8,128)} %all-gather.15.cloned.1.call-done, f32[4096,512]{1,0:T(8,128)} %all-gather.17.cloned.1.call-done), kind=kOutput, calls=%fused_computation.8 | convolution fusion | flops 6442975232 | bytes 14155777 | tf_op jit(solution)/shard_map/dot_general | solution.py:28
  250.1 30.7 %all-gather.19.cloned.1.call-done = f32[256,4096]{1,0:T(8,128)} async-done(((f32[256,512]{1,0:T(8,128)}), f32[256,4096]{1,0:T(8,128)}) %all-gather.19.cloned.1.call-update) | async-done | bytes 4194320 | tf_op jit(solution)/shard_map/all_gather | solution.py:27
  280.8 72.0 %all-gather.21.cloned.1.call-done = f32[4096,512]{1,0:T(8,128)} async-done(((f32[256,512]{1,0:T(8,128)}), f32[4096,512]{1,0:T(8,128)}) %all-gather.21.cloned.1.call-update) | async-done | bytes 8388624 | tf_op jit(solution)/shard_map/all_gather | solution.py:30
  352.8 11.5 %fusion.2 = f32[256,512]{1,0:T(8,128)} fusion(f32[256,512]{1,0:T(8,128)S(1)} %copy.33, f32[256,512]{1,0:T(8,128)} %fusion.1, pred[]{:T(512)} %bitcast.2, f32[256,4096]{1,0:T(8,128)} %all-gather.19.cloned.1.call-done, f32[4096,512]{1,0:T(8,128)} %all-gather.21.cloned.1.call-done), kind=kOutput, calls=%fused_computation.9 | convolution fusion | flops 6442975232 | bytes 14155777 | tf_op jit(solution)/shard_map/dot_general | solution.py:28
  364.4 0.7 all-gather.25.cloned.1.call-update
  366.2 30.7 %all-gather.23.cloned.1.call-done = f32[256,4096]{1,0:T(8,128)} async-done(((f32[256,512]{1,0:T(8,128)}), f32[256,4096]{1,0:T(8,128)}) %all-gather.23.cloned.1.call-update) | async-done | bytes 4194320 | tf_op jit(solution)/shard_map/all_gather | solution.py:27
  397.0 72.2 %all-gather.25.cloned.1.call-done = f32[4096,512]{1,0:T(8,128)} async-done(((f32[256,512]{1,0:T(8,128)}), f32[4096,512]{1,0:T(8,128)}) %all-gather.25.cloned.1.call-update) | async-done | bytes 8388624 | tf_op jit(solution)/shard_map/all_gather | solution.py:30
  469.1 11.5 %fusion.3 = f32[256,512]{1,0:T(8,128)} fusion(f32[256,512]{1,0:T(8,128)S(1)} %copy.35, f32[256,512]{1,0:T(8,128)} %fusion.2, pred[]{:T(512)} %bitcast.1, f32[256,4096]{1,0:T(8,128)} %all-gather.23.cloned.1.call-done, f32[4096,512]{1,0:T(8,128)} %all-gather.25.cloned.1.call-done), kind=kOutput, calls=%fused_computation.10 | convolution fusion | flops 6442975232 | bytes 14155777 | tf_op jit(solution)/shard_map/dot_general | solution.py:28
  482.4 30.8 %all-gather.27.cloned.1.call-done = f32[256,4096]{1,0:T(8,128)} async-done(((f32[256,512]{1,0:T(8,128)}), f32[256,4096]{1,0:T(8,128)}) %all-gather.27.cloned.1.call-update) | async-done | bytes 4194320 | tf_op jit(solution)/shard_map/all_gather | solution.py:27
  513.2 72.0 %all-gather.29.cloned.1.call-done = f32[4096,512]{1,0:T(8,128)} async-done(((f32[256,512]{1,0:T(8,128)}), f32[4096,512]{1,0:T(8,128)}) %all-gather.29.cloned.1.call-update) | async-done | bytes 8388624 | tf_op jit(solution)/shard_map/all_gather | solution.py:30
  585.3 11.5 %fusion.4 = f32[256,512]{1,0:T(8,128)} fusion(f32[256,512]{1,0:T(8,128)S(1)} %copy.37, f32[256,512]{1,0:T(8,128)} %fusion.3, pred[]{:T(512)} %bitcast, f32[256,4096]{1,0:T(8,128)} %all-gather.27.cloned.1.call-done, f32[4096,512]{1,0:T(8,128)} %all-gather.29.cloned.1.call-done), kind=kOutput, calls=%fused_computation.11 | convolution fusion | flops 6442975232 | bytes 14155777 | tf_op jit(solution)/shard_map/dot_general | solution.py:28
  (58 shorter events, 5.1 us)
Async XLA Ops:
  6.5 0.9 copy-start
  6.5 41.8 %all-gather.11.cloned.1.call-start = ((), (), s32[]{:S(2)}) async-start(), calls=%async_computation | async-start | bytes 4718592 | tf_op jit(solution)/shard_map/all_gather | solution.py:27
  12.2 108.3 %all-gather.13.cloned.1.call-start = ((), (), s32[]{:S(2)}) async-start(), calls=%async_computation.1 | async-start | bytes 8912896 | tf_op jit(solution)/shard_map/all_gather | solution.py:30
  12.9 151.7 %all-gather.15.cloned.1.call-start = ((), (), s32[]{:S(2)}) async-start(), calls=%async_computation.2 | async-start | bytes 4718592 | tf_op jit(solution)/shard_map/all_gather | solution.py:27
  132.0 104.7 %all-gather.17.cloned.1.call-start = ((), (), s32[]{:S(2)}) async-start(), calls=%async_computation.3 | async-start | bytes 8912896 | tf_op jit(solution)/shard_map/all_gather | solution.py:30
  132.6 148.2 %all-gather.19.cloned.1.call-start = ((), (), s32[]{:S(2)}) async-start(), calls=%async_computation.4 | async-start | bytes 4718592 | tf_op jit(solution)/shard_map/all_gather | solution.py:27
  248.1 104.7 %all-gather.21.cloned.1.call-start = ((), (), s32[]{:S(2)}) async-start(), calls=%async_computation.5 | async-start | bytes 8912896 | tf_op jit(solution)/shard_map/all_gather | solution.py:30
  248.7 148.3 %all-gather.23.cloned.1.call-start = ((), (), s32[]{:S(2)}) async-start(), calls=%async_computation.6 | async-start | bytes 4718592 | tf_op jit(solution)/shard_map/all_gather | solution.py:27
  364.3 104.8 %all-gather.25.cloned.1.call-start = ((), (), s32[]{:S(2)}) async-start(), calls=%async_computation.7 | async-start | bytes 8912896 | tf_op jit(solution)/shard_map/all_gather | solution.py:30
  365.1 148.2 %all-gather.27.cloned.1.call-start = ((), (), s32[]{:S(2)}) async-start(), calls=%async_computation.8 | async-start | bytes 4718592 | tf_op jit(solution)/shard_map/all_gather | solution.py:27
  480.6 116.1 %copy-start.1 = (s32[6,64,64]{2,1,0:T(8,128)S(1)}, s32[6,64,64]{2,1,0:T(8,128)}, u32[]{:S(2)}) copy-start(s32[6,64,64]{2,1,0:T(8,128)} %param.5) | copy-start | bytes 294916
  480.6 104.6 %all-gather.29.cloned.1.call-start = ((), (), s32[]{:S(2)}) async-start(), calls=%async_computation.9 | async-start | bytes 8912896 | tf_op jit(solution)/shard_map/all_gather | solution.py:30
Sparse Core Ops, SparseCore 0:
  12.3 35.9 all-gather.10
  50.5 69.9 all-gather.12
  132.1 32.4 all-gather.14
  166.6 69.9 all-gather.16
  248.3 32.5 all-gather.18
  282.8 69.9 all-gather.20
  364.4 32.4 all-gather.22
  399.1 69.9 all-gather.24
  480.7 32.4 all-gather.26
  515.2 69.9 all-gather.28
where the time goes:
time: 604 us
  waiting for transfers between devices  519 us (86%)
  matrix products  57.3 us (9%)
  between operations  16.9 us (3%)
    all_gather x5, waiting for transfers between devices, shards(): lax.all_gather(current, 'row', axis=0, tiled=True)  360 us
    all_gather x5, waiting for transfers between devices, shards(): panel = lax.all_gather(current, ('col', 'layer'), axis=1, tiled=True)  156 us
    dot_general x5, matrix products, shards(): jnp.dot(panel, lax.all_gather(current, 'row', axis=0, tiled=True), prefer...  57.3 us
  transfers between devices with their start and end apart: 10, of which 10 were waited for; matrix products, arithmetic and copies ran while one was open for 1% of the time, Pallas kernels for 0%

commit v1 on v0

--- a/solution.py
+++ b/solution.py
@@ -5,6 +5,12 @@
 
 BS = 64
 STEPS = 5
+
+
+def tiled_gather(x, axis, dim):
+    peers = lax.axis_size(axis)
+    repeats = [peers if d == dim else 1 for d in range(x.ndim)]
+    return lax.all_to_all(jnp.tile(x, repeats), axis, split_axis=dim, concat_axis=dim, tiled=True)
 
 
 def expand(block_mask):
@@ -27,7 +33,7 @@
         panel = lax.all_gather(current, ("col", "layer"), axis=1, tiled=True)
         square = jnp.dot(
             panel,
-            lax.all_gather(current, "row", axis=0, tiled=True),
+            tiled_gather(current, "row", 0),
             preferred_element_type=jnp.float32,
             precision=lax.Precision.HIGHEST,
         )

time: 604 us -> 745 us (1.23)
  the two profiles are of different devices: /device:TPU:1 before, /device:TPU:124 now
where the time goes in v1:
time: 745 us; the launch traced here: 744 us
  waiting for transfers between devices  607 us (81%)
  matrix products  55.6 us (7%)
  starting transfers between devices  35.6 us (5%)
  local copies, waits for them, and re-layouts  26.8 us (4%)
  between operations  16.6 us (2%)
    all_to_all x5, waiting for transfers between devices, tiled_gather(): lax.all_to_all(jnp.tile(x, repeats), axis, split_axis=dim, concat_axis=di...  445 us
    all_gather x5, waiting for transfers between devices, shards(): panel = lax.all_gather(current, ('col', 'layer'), axis=1, tiled=True)  159 us
    dot_general x5, matrix products, shards(): jnp.dot(panel, tiled_gather(current, 'row', 0), preferred_element_type=jn...  55.6 us
    all_to_all x5, starting transfers between devices, tiled_gather(): lax.all_to_all(jnp.tile(x, repeats), axis, split_axis=dim, concat_axis=di...  35 us
    another operation x5, local copies, waits for them, and re-layouts, tiled_gather(): jnp.tile(x, repeats)  21.7 us
  transfers between devices with their start and end apart: 10, of which 10 were waited for; matrix products, arithmetic and copies ran while one was open for 0% of the time, Pallas kernels for 0%

profile of v1, /device:TPU:124, one launch (start us, length us, event | category | flops | bytes accessed | tf_op | source)
XLA Modules:
  0.0 743.9 jit_solution(14752514617441286529)
XLA Ops:
  11.4 4.3 tile.10
  15.7 7.2 all-to-all-start
  25.5 31.3 %all-gather.6.cloned.1.call-done = f32[256,4096]{1,0:T(8,128)} async-done(((f32[256,512]{1,0:T(8,128)}), f32[256,4096]{1,0:T(8,128)}) %all-gather.6.cloned.1.call-update) | async-done | bytes 4194320 | tf_op jit(solution)/shard_map/all_gather | solution.py:33
  56.7 115.3 %all-to-all-done = f32[16,256,512]{2,1,0:T(8,128)} async-done(((f32[16,256,512]{2,1,0:T(8,128)}), f32[16,256,512]{2,1,0:T(8,128)}, u32[]{:S(2)}, u32[]{:S(2)}) %all-to-all-start) | async-done | bytes 8388640 | tf_op jit(solution)/shard_map/all_to_all | solution.py:13
  172.1 11.0 %fusion = f32[256,512]{1,0:T(8,128)S(1)} fusion(f32[256,512]{1,0:T(8,128)S(1)} %copy.29, f32[256,512]{1,0:T(8,128)} %copy-done.3, pred[]{:T(512)} %bitcast.4, f32[256,4096]{1,0:T(8,128)} %all-gather.6.cloned.1.call-done, f32[4096,512]{1,0:T(8,128)} %bitcast.9), kind=kOutput, calls=%fused_computation.7 | convolution fusion | flops 6442975232 | bytes 14155777 | tf_op jit(solution)/shard_map/dot_general | solution.py:34
  183.1 4.3 tile.11
  187.5 6.9 all-to-all-start.1
  196.3 31.9 %all-gather.8.cloned.1.call-done = f32[256,4096]{1,0:T(8,128)} async-done(((f32[256,512]{1,0:T(8,128)}), f32[256,4096]{1,0:T(8,128)}) %all-gather.8.cloned.1.call-update) | async-done | bytes 4194320 | tf_op jit(solution)/shard_map/all_gather | solution.py:33
  228.2 100.5 %all-to-all-done.1 = f32[16,256,512]{2,1,0:T(8,128)} async-done(((f32[16,256,512]{2,1,0:T(8,128)}), f32[16,256,512]{2,1,0:T(8,128)}, u32[]{:S(2)}, u32[]{:S(2)}) %all-to-all-start.1) | async-done | bytes 8388640 | tf_op jit(solution)/shard_map/all_to_all | solution.py:13
  328.7 11.0 %fusion.1 = f32[256,512]{1,0:T(8,128)S(1)} fusion(f32[256,512]{1,0:T(8,128)S(1)} %copy.31, f32[256,512]{1,0:T(8,128)} %copy-done.4, pred[]{:T(512)} %bitcast.3, f32[256,4096]{1,0:T(8,128)} %all-gather.8.cloned.1.call-done, f32[4096,512]{1,0:T(8,128)} %bitcast.12), kind=kOutput, calls=%fused_computation.8 | convolution fusion | flops 6442975232 | bytes 14155777 | tf_op jit(solution)/shard_map/dot_general | solution.py:34
  339.7 4.3 tile.12
  344.1 6.9 all-to-all-start.2
  352.9 31.9 %all-gather.10.cloned.1.call-done = f32[256,4096]{1,0:T(8,128)} async-done(((f32[256,512]{1,0:T(8,128)}), f32[256,4096]{1,0:T(8,128)}) %all-gather.10.cloned.1.call-update) | async-done | bytes 4194320 | tf_op jit(solution)/shard_map/all_gather | solution.py:33
  384.8 86.8 %all-to-all-done.2 = f32[16,256,512]{2,1,0:T(8,128)} async-done(((f32[16,256,512]{2,1,0:T(8,128)}), f32[16,256,512]{2,1,0:T(8,128)}, u32[]{:S(2)}, u32[]{:S(2)}) %all-to-all-start.2) | async-done | bytes 8388640 | tf_op jit(solution)/shard_map/all_to_all | solution.py:13
  471.6 11.0 %fusion.2 = f32[256,512]{1,0:T(8,128)S(1)} fusion(f32[256,512]{1,0:T(8,128)S(1)} %copy.33, f32[256,512]{1,0:T(8,128)} %copy-done.5, pred[]{:T(512)} %bitcast.2, f32[256,4096]{1,0:T(8,128)} %all-gather.10.cloned.1.call-done, f32[4096,512]{1,0:T(8,128)} %bitcast.15), kind=kOutput, calls=%fused_computation.9 | convolution fusion | flops 6442975232 | bytes 14155777 | tf_op jit(solution)/shard_map/dot_general | solution.py:34
  487.0 6.9 all-to-all-start.3
  495.7 31.8 %all-gather.12.cloned.1.call-done = f32[256,4096]{1,0:T(8,128)} async-done(((f32[256,512]{1,0:T(8,128)}), f32[256,4096]{1,0:T(8,128)}) %all-gather.12.cloned.1.call-update) | async-done | bytes 4194320 | tf_op jit(solution)/shard_map/all_gather | solution.py:33
  527.5 64.7 %all-to-all-done.3 = f32[16,256,512]{2,1,0:T(8,128)} async-done(((f32[16,256,512]{2,1,0:T(8,128)}), f32[16,256,512]{2,1,0:T(8,128)}, u32[]{:S(2)}, u32[]{:S(2)}) %all-to-all-start.3) | async-done | bytes 8388640 | tf_op jit(solution)/shard_map/all_to_all | solution.py:13
  592.1 11.0 %fusion.3 = f32[256,512]{1,0:T(8,128)S(1)} fusion(f32[256,512]{1,0:T(8,128)S(1)} %copy.35, f32[256,512]{1,0:T(8,128)} %copy-done.6, pred[]{:T(512)} %bitcast.1, f32[256,4096]{1,0:T(8,128)} %all-gather.12.cloned.1.call-done, f32[4096,512]{1,0:T(8,128)} %bitcast.18), kind=kOutput, calls=%fused_computation.10 | convolution fusion | flops 6442975232 | bytes 14155777 | tf_op jit(solution)/shard_map/dot_general | solution.py:34
  603.2 4.3 tile.14
  607.5 6.9 all-to-all-start.4
  616.2 31.8 %all-gather.14.cloned.1.call-done = f32[256,4096]{1,0:T(8,128)} async-done(((f32[256,512]{1,0:T(8,128)}), f32[256,4096]{1,0:T(8,128)}) %all-gather.14.cloned.1.call-update) | async-done | bytes 4194320 | tf_op jit(solution)/shard_map/all_gather | solution.py:33
  647.9 78.0 %all-to-all-done.4 = f32[16,256,512]{2,1,0:T(8,128)} async-done(((f32[16,256,512]{2,1,0:T(8,128)}), f32[16,256,512]{2,1,0:T(8,128)}, u32[]{:S(2)}, u32[]{:S(2)}) %all-to-all-start.4) | async-done | bytes 8388640 | tf_op jit(solution)/shard_map/all_to_all | solution.py:13
  725.9 11.5 %fusion.4 = f32[256,512]{1,0:T(8,128)} fusion(f32[256,512]{1,0:T(8,128)S(1)} %copy.37, f32[256,512]{1,0:T(8,128)} %copy-done.2, pred[]{:T(512)} %bitcast, f32[256,4096]{1,0:T(8,128)} %all-gather.14.cloned.1.call-done, f32[4096,512]{1,0:T(8,128)} %bitcast.21), kind=kOutput, calls=%fused_computation.11 | convolution fusion | flops 6442975232 | bytes 14155777 | tf_op jit(solution)/shard_map/dot_general | solution.py:34
  (70 shorter events, 15.5 us)
Async XLA Ops:
  6.5 0.9 copy-start
  11.3 4.4 copy-start.3
  15.7 8.5 %copy-start.7 = (s32[5]{0:T(128)S(1)}, s32[5]{0:T(128)}, u32[]{:S(2)}) copy-start(s32[5]{0:T(128)} %param.6) | copy-start | bytes 64
  15.7 156.4 %all-to-all-start = ((f32[16,256,512]{2,1,0:T(8,128)}), f32[16,256,512]{2,1,0:T(8,128)}, u32[]{:S(2)}, u32[]{:S(2)}) async-start(f32[16,256,512]{2,1,0:T(8,128)} %tile.10), calls=%async_computation | async-start | bytes 16777216 | tf_op jit(solution)/shard_map/all_to_all | solution.py:13
  22.9 33.8 %all-gather.6.cloned.1.call-start = ((), (), s32[]{:S(2)}) async-start(), calls=%async_computation.5 | async-start | bytes 4718592 | tf_op jit(solution)/shard_map/all_gather | solution.py:33
  183.1 4.4 copy-start.4
  187.5 141.2 %all-to-all-start.1 = ((f32[16,256,512]{2,1,0:T(8,128)}), f32[16,256,512]{2,1,0:T(8,128)}, u32[]{:S(2)}, u32[]{:S(2)}) async-start(f32[16,256,512]{2,1,0:T(8,128)} %tile.11), calls=%async_computation.1 | async-start | bytes 16777216 | tf_op jit(solution)/shard_map/all_to_all | solution.py:13
  194.4 33.8 %all-gather.8.cloned.1.call-start = ((), (), s32[]{:S(2)}) async-start(), calls=%async_computation.6 | async-start | bytes 4718592 | tf_op jit(solution)/shard_map/all_gather | solution.py:33
  339.7 4.4 copy-start.5
  344.1 127.6 %all-to-all-start.2 = ((f32[16,256,512]{2,1,0:T(8,128)}), f32[16,256,512]{2,1,0:T(8,128)}, u32[]{:S(2)}, u32[]{:S(2)}) async-start(f32[16,256,512]{2,1,0:T(8,128)} %tile.12), calls=%async_computation.2 | async-start | bytes 16777216 | tf_op jit(solution)/shard_map/all_to_all | solution.py:13
  351.0 33.8 %all-gather.10.cloned.1.call-start = ((), (), s32[]{:S(2)}) async-start(), calls=%async_computation.7 | async-start | bytes 4718592 | tf_op jit(solution)/shard_map/all_gather | solution.py:33
  482.7 4.4 copy-start.6
  487.0 105.1 %all-to-all-start.3 = ((f32[16,256,512]{2,1,0:T(8,128)}), f32[16,256,512]{2,1,0:T(8,128)}, u32[]{:S(2)}, u32[]{:S(2)}) async-start(f32[16,256,512]{2,1,0:T(8,128)} %tile.13), calls=%async_computation.3 | async-start | bytes 16777216 | tf_op jit(solution)/shard_map/all_to_all | solution.py:13
  494.0 33.5 %all-gather.12.cloned.1.call-start = ((), (), s32[]{:S(2)}) async-start(), calls=%async_computation.8 | async-start | bytes 4718592 | tf_op jit(solution)/shard_map/all_gather | solution.py:33
  603.2 4.4 copy-start.2
  607.5 118.4 %all-to-all-start.4 = ((f32[16,256,512]{2,1,0:T(8,128)}), f32[16,256,512]{2,1,0:T(8,128)}, u32[]{:S(2)}, u32[]{:S(2)}) async-start(f32[16,256,512]{2,1,0:T(8,128)} %tile.14), calls=%async_computation.4 | async-start | bytes 16777216 | tf_op jit(solution)/shard_map/all_to_all | solution.py:13
  614.4 122.9 %copy-start.1 = (s32[6,64,64]{2,1,0:T(8,128)S(1)}, s32[6,64,64]{2,1,0:T(8,128)}, u32[]{:S(2)}) copy-start(s32[6,64,64]{2,1,0:T(8,128)} %param.5) | copy-start | bytes 294916
  614.4 33.5 %all-gather.14.cloned.1.call-start = ((), (), s32[]{:S(2)}) async-start(), calls=%async_computation.9 | async-start | bytes 4718592 | tf_op jit(solution)/shard_map/all_gather | solution.py:33
Sparse Core Ops, SparseCore 0:
  25.5 31.2 all-gather.5
  196.9 31.2 all-gather.7
  353.5 31.2 all-gather.9
  496.2 31.2 all-gather.11
  616.7 31.2 all-gather.13
